TPU v7x, 512 devices: a whole 4x8x8 slice. The times are simulated.
512 devices in a mesh: row: 32 (over z, y_lo), col: 4 (over y_hi, core), head: 4 (over x).
Axes of the slice: x: 4, y: 8 (y_hi: 2, y_lo: 4; y = y_hi * 4 + y_lo), z: 8, core: 2. Of those that a mesh axis runs over, the one named last changes fastest.
Arguments:
- tokens: bfloat16 [512, 128, 1024], P(('row', 'head'), 'col'), may hold values from -6 to 6
- valid: int32 [512, 128], P('row', 'col'), may hold values 0 or 1
- gain: float32 [1024], replicated, may hold values from 0.1 to 1.9
- w_qkv: bfloat16 [1024, 3, 1024], P(None, None, 'head'), may hold values from -0.1875 to 0.1875
- w_proj: bfloat16 [1024, 1024], P('head'), may hold values from -0.1875 to 0.1875
- rel_table: float32 [225, 16], P(None, 'head'), may hold values from -4 to 300
- cotangent: bfloat16 [512, 128, 1024], P(('row', 'head'), 'col'), may hold values from -24 to 24
Outputs:
- mixed: bfloat16 [512, 128, 1024], P(('row', 'head'), 'col')
- token_gradient: bfloat16 [512, 128, 1024], P(('row', 'head'), 'col')
- proj_grad: float32 [1024, 1024], P('head', ('row', 'col'))
- table_grad: float32 [225, 16], P(None, 'head')
All inputs are finite; a program needn't handle non-finite values. No bound on the sum of `valid` on one device may be relied on, other than what follows from the above.
Results may differ from a plain program's by a relative error of at most 0.0078.
Values may be sent and summed in bfloat16 or wider, within the bound.
No kernel may reach another device: no remote copies, remote signals or barrier semaphores. Data moves between devices by JAX's collectives and lax.ppermute only.
A program may use at most 64 MiB of HBM per device.

v0:
```python
import math
import jax
import jax.numpy as jnp
from jax import lax
from jax.sharding import PartitionSpec as P

HD = 64
WIN = 8
SHIFT = 4
EPS = 1e-05
HIGH = lax.Precision.HIGHEST


def passed_along(value, axis, steps):
    count = lax.axis_size(axis)
    pairs = [(source, (source + steps) % count) for source in range(count)]
    return lax.ppermute(value, axis, pairs)


def region(index, grand_total):
    return jnp.where(
        index < grand_total - WIN, 0, jnp.where(index < grand_total - SHIFT, 1, 2)
    ).astype(jnp.int32)


def offsets():
    span = 2 * WIN - 1
    pos = jnp.arange(WIN * WIN, dtype=jnp.int32)
    prow = pos // WIN
    pcol = pos % WIN
    index = (prow[:, None] - prow[None, :] + WIN - 1) * span + (
        pcol[:, None] - pcol[None, :] + WIN - 1
    )
    table_ids = jnp.arange(span * span, dtype=jnp.int32)
    return (
        (index[:, :, None] == table_ids[None, None, :])
        .astype(jnp.float32)
        .reshape(WIN * WIN * WIN * WIN, span * span)
    )


def to_windows(block):
    nrow, ncol, heads, depth = block.shape
    block = block.reshape(nrow // WIN, WIN, ncol // WIN, WIN, heads, depth).transpose(
        0, 2, 4, 1, 3, 5
    )
    return block.reshape(nrow // WIN * (ncol // WIN), heads, WIN * WIN, depth)


def from_windows(block, nrow, ncol):
    count, heads, posn, depth = block.shape
    block = block.reshape(nrow // WIN, ncol // WIN, heads, WIN, WIN, depth).transpose(
        0, 3, 1, 4, 2, 5
    )
    return block.reshape(nrow, ncol, heads * depth)


def rows_in(block):
    return jnp.concatenate([block[SHIFT:], passed_along(block[:SHIFT], "row", -1)], 0)


def cols_in(block):
    return jnp.concatenate([block[:, SHIFT:], passed_along(block[:, :SHIFT], "col", -1)], 1)


def rows_out(block):
    return jnp.concatenate([passed_along(block[-SHIFT:], "row", 1), block[:-SHIFT]], 0)


def cols_out(block):
    return jnp.concatenate([passed_along(block[:, -SHIFT:], "col", 1), block[:, :-SHIFT]], 1)


def roll_in(block):
    return cols_in(rows_in(block))


def roll_out(block):
    return cols_out(rows_out(block))


def roll_pair(first, second, roller):
    return (roller(first), roller(second))


def head_sum(term_fn, part_rows):
    return lax.psum_scatter(
        term_fn(jnp.int32(0), lax.axis_size("head") * part_rows).astype(jnp.bfloat16),
        "head",
        scatter_dimension=0,
        tiled=True,
    ).astype(jnp.float32)


def attend(qkv, grad, labels, valid, bias, onehot):
    nrow, ncol = labels.shape
    feature_width = qkv.shape[3]
    heads = feature_width // HD
    scale = HD ** (-0.5)
    f32 = jnp.float32
    query = to_windows(qkv[:, :, 0].reshape(nrow, ncol, heads, HD))
    key = to_windows(qkv[:, :, 1].reshape(nrow, ncol, heads, HD))
    value = to_windows(qkv[:, :, 2].reshape(nrow, ncol, heads, HD))
    dout = to_windows(grad.reshape(nrow, ncol, heads, HD))
    lab_win = to_windows(labels[:, :, None, None])[:, 0, :, 0]
    val_win = to_windows(valid[:, :, None, None])[:, 0, :, 0]
    diagonal = jnp.eye(WIN * WIN, dtype=bool)
    allowed = (lab_win[:, :, None] == lab_win[:, None, :]) & (
        (val_win[:, None, :] == 1) | diagonal[None]
    )
    scores = (
        jnp.einsum("wiqd,wikd->wiqk", query, key, preferred_element_type=f32) * scale + bias[None]
    )
    scores = jnp.where(allowed[:, None], scores, -1e30)
    top = jnp.max(scores, -1, keepdims=True)
    expo = jnp.exp(scores - top)
    prob = expo / jnp.sum(expo, -1, keepdims=True)
    prob_b = prob.astype(jnp.bfloat16)
    attended = jnp.einsum("wiqk,wikd->wiqd", prob_b, value, preferred_element_type=f32).astype(
        jnp.bfloat16
    )
    dprob = jnp.einsum("wiqd,wikd->wiqk", dout, value, preferred_element_type=f32)
    dvalue = jnp.einsum("wiqk,wiqd->wikd", prob_b, dout, preferred_element_type=f32).astype(
        jnp.bfloat16
    )
    dscore = prob * (dprob - jnp.sum(prob * dprob, -1, keepdims=True))
    dscore_b = dscore.astype(jnp.bfloat16)
    dquery = (
        jnp.einsum("wiqk,wikd->wiqd", dscore_b, key, preferred_element_type=f32) * scale
    ).astype(jnp.bfloat16)
    dkey = (
        jnp.einsum("wiqk,wiqd->wikd", dscore_b, query, preferred_element_type=f32) * scale
    ).astype(jnp.bfloat16)
    summed = jnp.sum(dscore, 0).transpose(1, 2, 0).reshape(WIN * WIN * WIN * WIN, heads)
    tgrad = jnp.dot(onehot.T, summed, precision=HIGH)
    grads = jnp.stack(
        [
            from_windows(dquery, nrow, ncol),
            from_windows(dkey, nrow, ncol),
            from_windows(dvalue, nrow, ncol),
        ],
        2,
    )
    return (from_windows(attended, nrow, ncol), grads, tgrad)


def on_device(tokens, valid, gain, w_qkv, w_proj, rel_table, cotangent):
    part_rows, ncol, feature_width = tokens.shape
    tile_rows = part_rows * lax.axis_size("head")
    row_count = lax.axis_size("row")
    col_count = lax.axis_size("col")
    flat = tokens.astype(jnp.float32)
    token_average = jnp.mean(flat, -1, keepdims=True)
    centered_input = flat - token_average
    inverse_deviation = lax.rsqrt(
        jnp.mean(centered_input * centered_input, -1, keepdims=True) + EPS
    )
    standardized_input = centered_input * inverse_deviation
    normalized_tokens = (standardized_input * gain).astype(jnp.bfloat16)
    grad_tile = lax.all_gather(cotangent, "head", axis=0, tiled=True)
    out_grad = jnp.einsum(
        "rcd,nd->rcn", grad_tile, w_proj, preferred_element_type=jnp.float32
    ).astype(jnp.bfloat16)
    source = lax.all_gather(normalized_tokens, "head", axis=0, tiled=True)
    moved, rolled_grad = roll_pair(source, out_grad, roll_in)
    rolled = jnp.einsum("rcd,dtn->rctn", moved, w_qkv, preferred_element_type=jnp.float32).astype(
        jnp.bfloat16
    )
    row_lab = region(
        lax.axis_index("row") * tile_rows + jnp.arange(tile_rows, dtype=jnp.int32),
        tile_rows * row_count,
    )
    col_lab = region(
        lax.axis_index("col") * ncol + jnp.arange(ncol, dtype=jnp.int32), ncol * col_count
    )
    labels = 3 * row_lab[:, None] + col_lab[None, :]
    onehot = offsets()
    heads = rel_table.shape[1]
    bias = (
        jnp.dot(onehot, rel_table, precision=HIGH)
        .reshape(WIN * WIN, WIN * WIN, heads)
        .transpose(2, 0, 1)
    )
    attended, grads, tgrad = attend(rolled, rolled_grad, labels, valid, bias, onehot)
    attn_out, qkv_grad = roll_pair(attended, grads, roll_out)

    def proj_term(start, count):
        return jnp.einsum("rcn,nd->rcd", attn_out, w_proj, preferred_element_type=jnp.float32)

    def back_term(start, count):
        return jnp.einsum("rctn,dtn->rcd", qkv_grad, w_qkv, preferred_element_type=jnp.float32)

    mixed = (flat + head_sum(proj_term, part_rows)).astype(jnp.bfloat16)
    norm_grad = head_sum(back_term, part_rows)
    scale = 1.0 / math.sqrt(tile_rows * ncol * row_count * col_count)
    weight_term = jnp.einsum("rcn,rcd->nd", attn_out, grad_tile, preferred_element_type=jnp.float32)
    proj_grad = (
        lax.psum_scatter(weight_term, ("row", "col"), scatter_dimension=1, tiled=True) * scale
    )
    table_grad = lax.psum(tgrad, ("row", "col")) * (WIN * scale)
    scaled_tokens = norm_grad * gain
    token_gradient = cotangent.astype(jnp.float32) + inverse_deviation * (
        scaled_tokens
        - jnp.mean(scaled_tokens, -1, keepdims=True)
        - standardized_input * jnp.mean(scaled_tokens * standardized_input, -1, keepdims=True)
    )
    return (mixed, token_gradient.astype(jnp.bfloat16), proj_grad, table_grad)


def solution(mesh):
    return jax.shard_map(
        on_device,
        mesh=mesh,
        in_specs=(
            P(("row", "head"), "col", None),
            P("row", "col"),
            P(),
            P(None, None, "head"),
            P("head", None),
            P(None, "head"),
            P(("row", "head"), "col", None),
        ),
        out_specs=(
            P(("row", "head"), "col", None),
            P(("row", "head"), "col", None),
            P("head", ("row", "col")),
            P(None, "head"),
        ),
        check_vma=False,
    )
```

profile of v0, /device:TPU:8, one launch (start us, length us, event | category | flops | bytes accessed | tf_op | source)
XLA Modules:
  0.0 753.7 jit_solution(1386446947580851297)
XLA Ops:
  14.0 3.4 fusion.17
  17.5 28.7 %all-gather.3.cloned.1.call-done = bf16[16,32,1024]{2,1,0:T(8,128)(2,1)} async-done(((bf16[4,32,1024]{2,1,0:T(8,128)(2,1)}), bf16[16,32,1024]{2,1,0:T(8,128)(2,1)}) %all-gather.3.cloned.1.call-update) | async-done | bytes 1048592 | tf_op jit(solution)/shard_map/all_gather | solution.py:164
  47.9 2.4 collective-permute-start
  50.4 27.6 %all-gather.5.cloned.1.call-done = bf16[16,32,1024]{2,1,0:T(8,128)(2,1)} async-done(((bf16[4,32,1024]{2,1,0:T(8,128)(2,1)}), bf16[16,32,1024]{2,1,0:T(8,128)(2,1)}) %all-gather.5.cloned.1.call-update) | async-done | bytes 1048592 | tf_op jit(solution)/shard_map/all_gather | solution.py:160
  79.7 2.4 collective-permute-start.4
  86.5 4.2 collective-permute-start.5
  91.5 4.3 collective-permute-start.1
  96.1 2.2 collective-permute-done.1
  106.7 3.0 convolution_convert_fusion.2
  113.3 2.5 collective-permute-start.2
  120.9 4.4 collective-permute-start.3
  125.4 2.9 convolution_convert_fusion.1
  131.1 2.8 convolution_bitcast_fusion
  140.4 2.2 stack_reshape.10
  144.4 6.4 collective-permute-start.6
  150.8 7.1 collective-permute-done.6
  157.9 2.4 collective-permute-start.7
  160.3 7.9 %collective-permute-done.7 = bf16[16,4,3,256]{3,1,2,0:T(4,128)(2,1)S(1)} collective-permute-done((bf16[16,4,3,256]{3,1,2,0:T(4,128)(2,1)S(1)}, bf16[16,4,3,256]{3,1,2,0:T(4,128)(2,1)S(1)}, u32[]{:S(2)}, u32[]{:S(2)}) %collective-permute-start.7) | collective-permute-done | bytes 98336 | tf_op jit(solution)/shard_map/ppermute | solution.py:17
  168.2 2.0 bitcast_convert_fusion
  173.4 266.7 %psum.7 = f32[225,4]{0,1:T(4,128)S(1)} all-reduce(f32[225,4]{0,1:T(4,128)S(1)} %fusion.18), channel_id=1, replica_groups=mesh['row'=32,'col'=4,'head'=4] {'row','col'}, use_global_device_ids=true, to_apply=%region_11.12 | all-reduce | flops 900 | bytes 7200 | tf_op jit(solution)/shard_map/psum | solution.py:200
  440.7 237.8 %reduce-scatter.8.cloned.1.call-done = f32[256,8]{0,1:T(8,128)} async-done(((f32[256,1024]{0,1:T(8,128)}), f32[256,8]{0,1:T(8,128)}) %reduce-scatter.8.cloned.1.call-update) | async-done | bytes 8208 | tf_op jit(solution)/shard_map/reduce_scatter | solution.py:198
  679.8 34.0 %reduce-scatter.6.cloned.1.call-done = bf16[4,32,1024]{2,1,0:T(8,128)(2,1)} async-done(((bf16[16,32,1024]{2,1,0:T(8,128)(2,1)}), bf16[4,32,1024]{2,1,0:T(8,128)(2,1)}) %reduce-scatter.6.cloned.1.call-update) | async-done | bytes 262160 | tf_op jit(solution)/shard_map/reduce_scatter | solution.py:87
  715.0 30.1 %reduce-scatter.4.cloned.1.call-done = bf16[4,32,1024]{2,1,0:T(8,128)(2,1)} async-done(((bf16[16,32,1024]{2,1,0:T(8,128)(2,1)}), bf16[4,32,1024]{2,1,0:T(8,128)(2,1)}) %reduce-scatter.4.cloned.1.call-update) | async-done | bytes 262160 | tf_op jit(solution)/shard_map/reduce_scatter | solution.py:87
  745.1 2.1 fusion.35
  (131 shorter events, 49.9 us)
Async XLA Ops:
  7.2 91.1 %copy-start = (bf16[1024,3,256]{2,0,1:T(8,128)(2,1)S(1)}, bf16[1024,3,256]{2,0,1:T(8,128)(2,1)}, u32[]{:S(2)}) copy-start(bf16[1024,3,256]{2,0,1:T(8,128)(2,1)} %param.10) | copy-start | bytes 4718596
  7.2 6.8 copy-start.22
  7.2 38.9 %all-gather.3.cloned.1.call-start = ((), (), s32[]{:S(2)}) async-start(), calls=%async_computation.3 | async-start | bytes 1310720 | tf_op jit(solution)/shard_map/all_gather | solution.py:164
  8.4 69.5 %copy-start.8 = (bf16[256,1024]{1,0:T(8,128)(2,1)S(1)}, bf16[256,1024]{1,0:T(8,128)(2,1)}, u32[]{:S(2)}) copy-start(bf16[256,1024]{1,0:T(8,128)(2,1)} %param.11) | copy-start | bytes 1572868
  12.1 65.8 %all-gather.5.cloned.1.call-start = ((), (), s32[]{:S(2)}) async-start(), calls=%async_computation.5 | async-start | bytes 1310720 | tf_op jit(solution)/shard_map/all_gather | solution.py:160
  12.9 665.6 %reduce-scatter.8.cloned.1.call-start = ((), (), s32[]{:S(2)}) async-start(), calls=%async_computation.7 | async-start | bytes 1056768 | tf_op jit(solution)/shard_map/reduce_scatter | solution.py:198
  46.1 38.2 %copy-start.6 = (bf16[16,32,1024]{2,1,0:T(8,128)(2,1)S(1)}, bf16[16,32,1024]{2,1,0:T(8,128)(2,1)}, u32[]{:S(2)}) copy-start(bf16[16,32,1024]{2,1,0:T(8,128)(2,1)} %all-gather.3.cloned.1.call-done) | copy-start | bytes 3145732
  47.9 43.5 %collective-permute-start = (bf16[4,32,1024]{2,1,0:T(8,128)(2,1)}, bf16[4,32,1024]{2,1,0:T(8,128)(2,1)S(1)}, u32[]{:S(2)}, u32[]{:S(2)}) collective-permute-start(bf16[4,32,1024]{2,1,0:T(8,128)(2,1)} %slice.77), channel_id=1, source_target_pairs={{0,496},{16,0},{32,16},{48,32},{64,48},{80,64},{96,80},{112,96},{1... | collective-permute-start | bytes 786440 | tf_op jit(solution)/shard_map/ppermute | solution.py:17
  79.7 6.2 collective-permute-start.4
  86.5 29.3 %collective-permute-start.5 = (bf16[16,4,256]{2,1,0:T(4,128)(2,1)}, bf16[16,4,256]{2,1,0:T(4,128)(2,1)}, u32[]{:S(2)}, u32[]{:S(2)}) collective-permute-start(bf16[16,4,256]{2,1,0:T(4,128)(2,1)} %pad_maximum_fusion.5), channel_id=1, source_target_pairs={{0,12},{4,0},{8,4},{12,8},{1,13},{5,1},{9,5},{13,9},{2,14},{6,2},{... | collective-permute-start | bytes 98312 | tf_op jit(solution)/shard_map/ppermute | solution.py:17
  91.5 6.8 collective-permute-start.1
  113.3 7.6 %collective-permute-start.2 = (bf16[4,32,256]{2,1,0:T(8,128)(2,1)S(1)}, bf16[4,32,256]{2,1,0:T(8,128)(2,1)S(1)}, u32[]{:S(2)}, u32[]{:S(2)}) collective-permute-start(bf16[4,32,256]{2,1,0:T(8,128)(2,1)S(1)} %slice.83), channel_id=1, source_target_pairs={{0,16},{16,32},{32,48},{48,64},{64,80},{80,96},{96,112},{112,128},... | collective-permute-start | bytes 196616 | tf_op jit(solution)/shard_map/ppermute | solution.py:17
  120.9 10.1 %collective-permute-start.3 = (bf16[16,4,256]{2,1,0:T(4,128)(2,1)S(1)}, bf16[16,4,256]{2,1,0:T(4,128)(2,1)S(1)}, u32[]{:S(2)}, u32[]{:S(2)}) collective-permute-start(bf16[16,4,256]{2,1,0:T(4,128)(2,1)S(1)} %pad_maximum_fusion.6), channel_id=1, source_target_pairs={{0,4},{4,8},{8,12},{12,0},{1,5},{5,9},{9,13},{13,1},{2,6},{6,10},{... | collective-permute-start | bytes 98312 | tf_op jit(solution)/shard_map/ppermute | solution.py:17
  133.9 579.8 %reduce-scatter.6.cloned.1.call-start = ((), (), s32[]{:S(2)}) async-start(), calls=%async_computation.6 | async-start | bytes 1310720 | tf_op jit(solution)/shard_map/reduce_scatter | solution.py:87
  144.4 13.5 %collective-permute-start.6 = (bf16[4,32,3,256]{3,1,2,0:T(8,128)(2,1)S(1)}, bf16[4,32,3,256]{3,1,2,0:T(8,128)(2,1)S(1)}, u32[]{:S(2)}, u32[]{:S(2)}) collective-permute-start(bf16[4,32,3,256]{3,1,2,0:T(8,128)(2,1)S(1)} %slice.89), channel_id=1, source_target_pairs={{0,16},{16,32},{32,48},{48,64},{64,80},{80,96},{96,112},{112,128},... | collective-permute-start | bytes 589832 | tf_op jit(solution)/shard_map/ppermute | solution.py:17
  157.9 12.4 %copy-start.9 = (bf16[256,1024]{1,0:T(8,128)(2,1)S(1)}, bf16[256,1024]{1,0:T(8,128)(2,1)}, u32[]{:S(2)}) copy-start(bf16[256,1024]{1,0:T(8,128)(2,1)} %param.11) | copy-start | bytes 1572868
  157.9 12.4 %copy-start.13 = (bf16[16,4,256]{2,1,0:T(4,128)(2,1)S(1)}, bf16[16,4,256]{2,1,0:T(4,128)(2,1)}, u32[]{:S(2)}) copy-start(bf16[16,4,256]{2,1,0:T(4,128)(2,1)} %copy-done.12) | copy-start | bytes 98308
  157.9 10.3 %collective-permute-start.7 = (bf16[16,4,3,256]{3,1,2,0:T(4,128)(2,1)S(1)}, bf16[16,4,3,256]{3,1,2,0:T(4,128)(2,1)S(1)}, u32[]{:S(2)}, u32[]{:S(2)}) collective-permute-start(bf16[16,4,3,256]{3,1,2,0:T(4,128)(2,1)S(1)} %pad_maximum_fusion.4), channel_id=1, source_target_pairs={{0,4},{4,8},{8,12},{12,0},{1,5},{5,9},{9,13},{13,1},{2,6},{6,10},{... | collective-permute-start | bytes 294920 | tf_op jit(solution)/shard_map/ppermute | solution.py:17
  170.3 574.9 %reduce-scatter.4.cloned.1.call-start = ((), (), s32[]{:S(2)}) async-start(), calls=%async_computation.4 | async-start | bytes 1310720 | tf_op jit(solution)/shard_map/reduce_scatter | solution.py:87
  171.8 542.0 %copy-start.1 = (bf16[4,32,1024]{2,1,0:T(8,128)(2,1)S(1)}, bf16[4,32,1024]{2,1,0:T(8,128)(2,1)}, u32[]{:S(2)}) copy-start(bf16[4,32,1024]{2,1,0:T(8,128)(2,1)} %param.7) | copy-start | bytes 786436
  171.8 542.0 %copy-start.15 = (f32[4,32]{1,0:T(4,128)S(1)}, f32[4,32]{1,0:T(4,128)}, u32[]{:S(2)}) copy-start(f32[4,32]{1,0:T(4,128)} %copy-done.14) | copy-start | bytes 1540
  171.8 542.0 %copy-start.16 = (f32[1024]{0:T(1024)S(1)}, f32[1024]{0:T(1024)}, u32[]{:S(2)}) copy-start(f32[1024]{0:T(1024)} %param.9) | copy-start | bytes 12292
  171.8 542.0 %copy-start.18 = (f32[4,32]{1,0:T(4,128)S(1)}, f32[4,32]{1,0:T(4,128)}, u32[]{:S(2)}) copy-start(f32[4,32]{1,0:T(4,128)} %copy-done.17) | copy-start | bytes 1540
  171.8 573.3 %copy-start.7 = (bf16[4,32,1024]{2,1,0:T(8,128)(2,1)S(1)}, bf16[4,32,1024]{2,1,0:T(8,128)(2,1)}, u32[]{:S(2)}) copy-start(bf16[4,32,1024]{2,1,0:T(8,128)(2,1)} %param.13) | copy-start | bytes 786436
  (12 other events, 23.8 us)
Sparse Core Ops, SparseCore 0:
  12.3 33.8 all-gather.2
  48.2 29.6 all-gather.4
  134.0 544.4 reduce-scatter.7
  681.4 32.2 reduce-scatter.5
  716.4 28.6 reduce-scatter.3
where the time goes:
time: 755 us; the launch traced here: 754 us
  waiting for transfers between devices  378 us (50%)
  blocking collectives  267 us (35%)
  starting transfers between devices  29.4 us (4%)
  local copies, waits for them, and re-layouts  26.9 us (4%)
  matrix products  23.6 us (3%)
  other arithmetic  14.9 us (2%)
  between operations  14.4 us (2%)
    psum x1, blocking collectives, on_device(): table_grad = lax.psum(tgrad, ('row', 'col')) * (WIN * scale)  267 us
    reduce_scatter x1, waiting for transfers between devices, on_device(): lax.psum_scatter(weight_term, ('row', 'col'), scatter_dimension=1, tiled=...  238 us
    reduce_scatter x2, waiting for transfers between devices, head_sum(): lax.psum_scatter(term_fn(jnp.int32(0), lax.axis_size('head') * part_rows)...  64.1 us
    ppermute x8, starting transfers between devices, passed_along(): return lax.ppermute(value, axis, pairs)  29 us
    all_gather x1, waiting for transfers between devices, on_device(): source = lax.all_gather(normalized_tokens, 'head', axis=0, tiled=True)  28.7 us
    all_gather x1, waiting for transfers between devices, on_device(): grad_tile = lax.all_gather(cotangent, 'head', axis=0, tiled=True)  27.6 us
    ppermute x8, waiting for transfers between devices, passed_along(): return lax.ppermute(value, axis, pairs)  19 us
  transfers between devices with their start and end apart: 13, of which 10 were waited for; matrix products, arithmetic and copies ran while one was open for 7% of the time, Pallas kernels for 0%

commit v1 on v0

--- a/solution.py
+++ b/solution.py
@@ -9,6 +9,28 @@
 SHIFT = 4
 EPS = 1e-05
 HIGH = lax.Precision.HIGHEST
+
+
+def laid_out(blocks, dim):
+    blocks = jnp.moveaxis(blocks, 0, dim)
+    shape = blocks.shape
+    return blocks.reshape(*shape[:dim], shape[dim] * shape[dim + 1], *shape[dim + 2 :])
+
+
+def gather_around(x, axis, dim):
+    peers = lax.axis_size(axis)
+    pairs = [(i, (i + 1) % peers) for i in range(peers)]
+    back = [(b, a) for a, b in pairs]
+    lower, upper = ([], [])
+    for turn in range(peers - 1):
+        if turn % 2 == 0:
+            lower.append(lax.ppermute(lower[-1] if lower else x, axis, pairs))
+        else:
+            upper.append(lax.ppermute(upper[-1] if upper else x, axis, back))
+    blocks = jnp.stack([*lower[::-1], x, *upper])
+    shift = lax.axis_index(axis) - len(lower)
+    blocks = blocks[(jnp.arange(peers) - shift) % peers]
+    return laid_out(blocks, dim)
 
 
 def passed_along(value, axis, steps):
@@ -157,7 +179,7 @@
     )
     standardized_input = centered_input * inverse_deviation
     normalized_tokens = (standardized_input * gain).astype(jnp.bfloat16)
-    grad_tile = lax.all_gather(cotangent, "head", axis=0, tiled=True)
+    grad_tile = gather_around(cotangent, "head", 0)
     out_grad = jnp.einsum(
         "rcd,nd->rcn", grad_tile, w_proj, preferred_element_type=jnp.float32
     ).astype(jnp.bfloat16)

time: 755 us -> 726 us (0.962)
  waiting for transfers between devices: 378 us -> 336 us
  starting transfers between devices: 29.4 us -> 39.1 us
    all_gather x1 -> x0, waiting for transfers between devices: 27.6 us -> none  [on_device(): grad_tile = lax.all_gather(cotangent, 'head', axis=0, tiled=True)]
    all_gather x1, waiting for transfers between devices: 28.7 us -> 10.5 us  [on_device(): source = lax.all_gather(normalized_tokens, 'head', axis=0, tiled=True)]
    ppermute x0 -> x3, starting transfers between devices: none -> 9.37 us  [the longest x2 5.71 us: gather_around(): lower.append(lax.ppermute(lower[-1] if lower else x, axis, pairs))]
  transfers between devices with their start and end apart: 13 -> 15, of which waited for: 10 -> 9; matrix products, arithmetic and copies ran while one was open for 7% -> 8% of each run, Pallas kernels for 0% -> 0%
where the time goes in v1:
time: 726 us; the launch traced here: 725 us
  waiting for transfers between devices  336 us (46%)
  blocking collectives  267 us (37%)
  starting transfers between devices  39.1 us (5%)
  local copies, waits for them, and re-layouts  24.5 us (3%)
  matrix products  23.9 us (3%)
  other arithmetic  19.5 us (3%)
  between operations  14.4 us (2%)
    psum x1, blocking collectives, on_device(): table_grad = lax.psum(tgrad, ('row', 'col')) * (WIN * scale)  267 us
    reduce_scatter x1, waiting for transfers between devices, on_device(): lax.psum_scatter(weight_term, ('row', 'col'), scatter_dimension=1, tiled=...  236 us
    reduce_scatter x2, waiting for transfers between devices, head_sum(): lax.psum_scatter(term_fn(jnp.int32(0), lax.axis_size('head') * part_rows)...  63.6 us
    ppermute x8, starting transfers between devices, passed_along(): return lax.ppermute(value, axis, pairs)  29.4 us
    ppermute x8, waiting for transfers between devices, passed_along(): return lax.ppermute(value, axis, pairs)  22.1 us
  transfers between devices with their start and end apart: 15, of which 9 were waited for; matrix products, arithmetic and copies ran while one was open for 8% of the time, Pallas kernels for 0%

profile of v1, /device:TPU:8, one launch (start us, length us, event | category | flops | bytes accessed | tf_op | source)
XLA Modules:
  0.0 725.1 jit_solution(6384101965422095429)
XLA Ops:
  7.2 3.5 collective-permute-start.4
  10.8 3.7 collective-permute-start.6
  20.2 2.2 collective-permute-start.5
  22.7 4.1 fusion.17
  26.8 4.0 collective-permute-done.5
  35.0 6.6 collective-permute-start.7
  41.6 10.5 %all-gather.2.cloned.1.call-done = bf16[16,32,1024]{2,1,0:T(8,128)(2,1)} async-done(((bf16[4,32,1024]{2,1,0:T(8,128)(2,1)}), bf16[16,32,1024]{2,1,0:T(8,128)(2,1)}) %all-gather.2.cloned.1.call-update) | async-done | bytes 1048592 | tf_op jit(solution)/shard_map/all_gather | solution.py:186
  53.0 2.4 collective-permute-start
  58.8 5.6 collective-permute-start.8
  66.2 3.8 collective-permute-start.1
  70.2 2.3 collective-permute-done.1
  80.7 2.9 convolution_convert_fusion.2
  85.8 2.4 collective-permute-start.2
  93.9 4.5 collective-permute-start.3
  98.3 2.9 convolution_convert_fusion.1
  104.0 2.8 convolution_bitcast_fusion
  114.0 2.2 stack_reshape.10
  120.0 11.1 %collective-permute-done.9 = bf16[4,32,3,256]{3,1,2,0:T(8,128)(2,1)S(1)} collective-permute-done((bf16[4,32,3,256]{3,1,2,0:T(8,128)(2,1)S(1)}, bf16[4,32,3,256]{3,1,2,0:T(8,128)(2,1)S(1)}, u32[]{:S(2)}, u32[]{:S(2)}) %collective-permute-start.9) | collective-permute-done | bytes 196640 | tf_op jit(solution)/shard_map/ppermute | solution.py:39
  131.1 2.2 collective-permute-start.10
  133.3 7.8 %collective-permute-done.10 = bf16[16,4,3,256]{3,1,2,0:T(4,128)(2,1)S(1)} collective-permute-done((bf16[16,4,3,256]{3,1,2,0:T(4,128)(2,1)S(1)}, bf16[16,4,3,256]{3,1,2,0:T(4,128)(2,1)S(1)}, u32[]{:S(2)}, u32[]{:S(2)}) %collective-permute-start.10) | collective-permute-done | bytes 98336 | tf_op jit(solution)/shard_map/ppermute | solution.py:39
  146.3 267.5 %psum.7 = f32[225,4]{0,1:T(4,128)S(1)} all-reduce(f32[225,4]{0,1:T(4,128)S(1)} %fusion.18), channel_id=1, replica_groups=mesh['row'=32,'col'=4,'head'=4] {'row','col'}, use_global_device_ids=true, to_apply=%region_11.12 | all-reduce | flops 900 | bytes 7200 | tf_op jit(solution)/shard_map/psum | solution.py:222
  414.4 236.0 %reduce-scatter.8.cloned.1.call-done = f32[256,8]{0,1:T(8,128)} async-done(((f32[256,1024]{0,1:T(8,128)}), f32[256,8]{0,1:T(8,128)}) %reduce-scatter.8.cloned.1.call-update) | async-done | bytes 8208 | tf_op jit(solution)/shard_map/reduce_scatter | solution.py:220
  651.6 33.4 %reduce-scatter.6.cloned.1.call-done = bf16[4,32,1024]{2,1,0:T(8,128)(2,1)} async-done(((bf16[16,32,1024]{2,1,0:T(8,128)(2,1)}), bf16[4,32,1024]{2,1,0:T(8,128)(2,1)}) %reduce-scatter.6.cloned.1.call-update) | async-done | bytes 262160 | tf_op jit(solution)/shard_map/reduce_scatter | solution.py:109
  686.3 30.2 %reduce-scatter.4.cloned.1.call-done = bf16[4,32,1024]{2,1,0:T(8,128)(2,1)} async-done(((bf16[16,32,1024]{2,1,0:T(8,128)(2,1)}), bf16[4,32,1024]{2,1,0:T(8,128)(2,1)}) %reduce-scatter.4.cloned.1.call-update) | async-done | bytes 262160 | tf_op jit(solution)/shard_map/reduce_scatter | solution.py:109
  (136 shorter events, 56.1 us)
Async XLA Ops:
  7.2 65.4 %copy-start = (bf16[1024,3,256]{2,0,1:T(8,128)(2,1)S(1)}, bf16[1024,3,256]{2,0,1:T(8,128)(2,1)}, u32[]{:S(2)}) copy-start(bf16[1024,3,256]{2,0,1:T(8,128)(2,1)} %param.10) | copy-start | bytes 4718596
  7.2 23.6 %copy-start.9 = (bf16[4,32,1024]{2,1,0:T(8,128)(2,1)S(1)}, bf16[4,32,1024]{2,1,0:T(8,128)(2,1)}, u32[]{:S(2)}) copy-start(bf16[4,32,1024]{2,1,0:T(8,128)(2,1)} %param.13) | copy-start | bytes 786436
  7.2 44.9 %all-gather.2.cloned.1.call-start = ((), (), s32[]{:S(2)}) async-start(), calls=%async_computation.3 | async-start | bytes 1310720 | tf_op jit(solution)/shard_map/all_gather | solution.py:186
  7.2 13.0 %collective-permute-start.4 = (bf16[4,32,1024]{2,1,0:T(8,128)(2,1)}, bf16[4,32,1024]{2,1,0:T(8,128)(2,1)S(1)}, u32[]{:S(2)}, u32[]{:S(2)}) collective-permute-start(bf16[4,32,1024]{2,1,0:T(8,128)(2,1)} %param.13), channel_id=1, source_target_pairs={{0,1},{1,2},{2,3},{3,0},{4,5},{5,6},{6,7},{7,4},{8,9},{9,10},{10,1... | collective-permute-start | bytes 786440 | tf_op jit(solution)/shard_map/ppermute | solution.py:27
  10.8 16.1 %collective-permute-start.6 = (bf16[4,32,1024]{2,1,0:T(8,128)(2,1)}, bf16[4,32,1024]{2,1,0:T(8,128)(2,1)S(1)}, u32[]{:S(2)}, u32[]{:S(2)}) collective-permute-start(bf16[4,32,1024]{2,1,0:T(8,128)(2,1)} %param.13), channel_id=1, source_target_pairs={{1,0},{2,1},{3,2},{0,3},{5,4},{6,5},{7,6},{4,7},{9,8},{10,9},{11,1... | collective-permute-start | bytes 786440 | tf_op jit(solution)/shard_map/ppermute | solution.py:29
  19.2 631.1 %reduce-scatter.8.cloned.1.call-start = ((), (), s32[]{:S(2)}) async-start(), calls=%async_computation.6 | async-start | bytes 1056768 | tf_op jit(solution)/shard_map/reduce_scatter | solution.py:220
  20.2 10.6 %collective-permute-start.5 = (bf16[4,32,1024]{2,1,0:T(8,128)(2,1)S(1)}, bf16[4,32,1024]{2,1,0:T(8,128)(2,1)S(1)}, u32[]{:S(2)}, u32[]{:S(2)}) collective-permute-start(bf16[4,32,1024]{2,1,0:T(8,128)(2,1)S(1)} %collective-permute-done.4), channel_id=1, source_target_pairs={{0,1},{1,2},{2,3},{3,0},{4,5},{5,6},{6,7},{7,4},{8,9},{9,10},{10,1... | collective-permute-start | bytes 786440 | tf_op jit(solution)/shard_map/ppermute | solution.py:27
  33.8 23.5 %copy-start.2 = (bf16[4,4,32,1024]{3,2,1,0:T(8,128)(2,1)}, bf16[4,4,32,1024]{3,2,1,0:T(8,128)(2,1)S(1)}, u32[]{:S(2)}) copy-start(bf16[4,4,32,1024]{3,2,1,0:T(8,128)(2,1)S(1)} %gather_fusion) | copy-start | bytes 3145732
  35.0 22.4 %collective-permute-start.7 = (bf16[4,32,256]{2,1,0:T(8,128)(2,1)}, bf16[4,32,256]{2,1,0:T(8,128)(2,1)}, u32[]{:S(2)}, u32[]{:S(2)}) collective-permute-start(bf16[4,32,256]{2,1,0:T(8,128)(2,1)} %slice.88), channel_id=1, source_target_pairs={{0,496},{16,0},{32,16},{48,32},{64,48},{80,64},{96,80},{112,96},{1... | collective-permute-start | bytes 196616 | tf_op jit(solution)/shard_map/ppermute | solution.py:39
  53.0 13.1 %collective-permute-start = (bf16[4,32,1024]{2,1,0:T(8,128)(2,1)S(1)}, bf16[4,32,1024]{2,1,0:T(8,128)(2,1)S(1)}, u32[]{:S(2)}, u32[]{:S(2)}) collective-permute-start(bf16[4,32,1024]{2,1,0:T(8,128)(2,1)S(1)} %slice.79), channel_id=1, source_target_pairs={{0,496},{16,0},{32,16},{48,32},{64,48},{80,64},{96,80},{112,96},{1... | collective-permute-start | bytes 786440 | tf_op jit(solution)/shard_map/ppermute | solution.py:39
  58.8 29.4 %collective-permute-start.8 = (bf16[16,4,256]{2,1,0:T(4,128)(2,1)}, bf16[16,4,256]{2,1,0:T(4,128)(2,1)}, u32[]{:S(2)}, u32[]{:S(2)}) collective-permute-start(bf16[16,4,256]{2,1,0:T(4,128)(2,1)} %pad_maximum_fusion.6), channel_id=1, source_target_pairs={{0,12},{4,0},{8,4},{12,8},{1,13},{5,1},{9,5},{13,9},{2,14},{6,2},{... | collective-permute-start | bytes 98312 | tf_op jit(solution)/shard_map/ppermute | solution.py:39
  66.2 6.4 collective-permute-start.1
  85.8 8.1 %collective-permute-start.2 = (bf16[4,32,256]{2,1,0:T(8,128)(2,1)S(1)}, bf16[4,32,256]{2,1,0:T(8,128)(2,1)S(1)}, u32[]{:S(2)}, u32[]{:S(2)}) collective-permute-start(bf16[4,32,256]{2,1,0:T(8,128)(2,1)S(1)} %slice.85), channel_id=1, source_target_pairs={{0,16},{16,32},{32,48},{48,64},{64,80},{80,96},{96,112},{112,128},... | collective-permute-start | bytes 196616 | tf_op jit(solution)/shard_map/ppermute | solution.py:39
  93.9 10.2 %collective-permute-start.3 = (bf16[16,4,256]{2,1,0:T(4,128)(2,1)S(1)}, bf16[16,4,256]{2,1,0:T(4,128)(2,1)S(1)}, u32[]{:S(2)}, u32[]{:S(2)}) collective-permute-start(bf16[16,4,256]{2,1,0:T(4,128)(2,1)S(1)} %pad_maximum_fusion.7), channel_id=1, source_target_pairs={{0,4},{4,8},{8,12},{12,0},{1,5},{5,9},{9,13},{13,1},{2,6},{6,10},{... | collective-permute-start | bytes 98312 | tf_op jit(solution)/shard_map/ppermute | solution.py:39
  106.9 578.2 %reduce-scatter.6.cloned.1.call-start = ((), (), s32[]{:S(2)}) async-start(), calls=%async_computation.5 | async-start | bytes 1310720 | tf_op jit(solution)/shard_map/reduce_scatter | solution.py:109
  118.0 13.1 %collective-permute-start.9 = (bf16[4,32,3,256]{3,1,2,0:T(8,128)(2,1)S(1)}, bf16[4,32,3,256]{3,1,2,0:T(8,128)(2,1)S(1)}, u32[]{:S(2)}, u32[]{:S(2)}) collective-permute-start(bf16[4,32,3,256]{3,1,2,0:T(8,128)(2,1)S(1)} %slice.91), channel_id=1, source_target_pairs={{0,16},{16,32},{32,48},{48,64},{64,80},{80,96},{96,112},{112,128},... | collective-permute-start | bytes 589832 | tf_op jit(solution)/shard_map/ppermute | solution.py:39
  131.1 12.2 %copy-start.12 = (bf16[256,1024]{1,0:T(8,128)(2,1)S(1)}, bf16[256,1024]{1,0:T(8,128)(2,1)}, u32[]{:S(2)}) copy-start(bf16[256,1024]{1,0:T(8,128)(2,1)} %param.11) | copy-start | bytes 1572868
  131.1 10.0 %collective-permute-start.10 = (bf16[16,4,3,256]{3,1,2,0:T(4,128)(2,1)S(1)}, bf16[16,4,3,256]{3,1,2,0:T(4,128)(2,1)S(1)}, u32[]{:S(2)}, u32[]{:S(2)}) collective-permute-start(bf16[16,4,3,256]{3,1,2,0:T(4,128)(2,1)S(1)} %pad_maximum_fusion.5), channel_id=1, source_target_pairs={{0,4},{4,8},{8,12},{12,0},{1,5},{5,9},{9,13},{13,1},{2,6},{6,10},{... | collective-permute-start | bytes 294920 | tf_op jit(solution)/shard_map/ppermute | solution.py:39
  143.2 573.2 %reduce-scatter.4.cloned.1.call-start = ((), (), s32[]{:S(2)}) async-start(), calls=%async_computation.4 | async-start | bytes 1310720 | tf_op jit(solution)/shard_map/reduce_scatter | solution.py:109
  144.7 540.3 %copy-start.1 = (bf16[4,32,1024]{2,1,0:T(8,128)(2,1)S(1)}, bf16[4,32,1024]{2,1,0:T(8,128)(2,1)}, u32[]{:S(2)}) copy-start(bf16[4,32,1024]{2,1,0:T(8,128)(2,1)} %param.7) | copy-start | bytes 786436
  144.7 540.4 %copy-start.16 = (f32[4,32]{1,0:T(4,128)S(1)}, f32[4,32]{1,0:T(4,128)}, u32[]{:S(2)}) copy-start(f32[4,32]{1,0:T(4,128)} %copy-done.15) | copy-start | bytes 1540
  144.7 540.4 %copy-start.17 = (f32[1024]{0:T(1024)S(1)}, f32[1024]{0:T(1024)}, u32[]{:S(2)}) copy-start(f32[1024]{0:T(1024)} %param.9) | copy-start | bytes 12292
  144.7 540.4 %copy-start.19 = (f32[4,32]{1,0:T(4,128)S(1)}, f32[4,32]{1,0:T(4,128)}, u32[]{:S(2)}) copy-start(f32[4,32]{1,0:T(4,128)} %copy-done.18) | copy-start | bytes 1540
  144.7 571.7 %copy-start.10 = (bf16[4,32,1024]{2,1,0:T(8,128)(2,1)S(1)}, bf16[4,32,1024]{2,1,0:T(8,128)(2,1)}, u32[]{:S(2)}) copy-start(bf16[4,32,1024]{2,1,0:T(8,128)(2,1)} %param.13) | copy-start | bytes 786436
  (13 other events, 40.2 us)
Sparse Core Ops, SparseCore 0:
  19.3 32.6 all-gather.1
  107.0 543.2 reduce-scatter.7
  653.4 31.6 reduce-scatter.5
  687.7 28.6 reduce-scatter.3
